TPU v7x, 256 devices: a whole 4x4x8 slice. The times are simulated.
256 devices in a mesh: section: 4 (over x), dp: 4 (over y), chan: 16 (over z, core).
Axes of the slice: x: 4, y: 4, z: 8, core: 2. Of those that a mesh axis runs over, the one named last changes fastest.
Arguments:
- feats: bfloat16 [8, 32, 128, 2048], P('dp', None, None, 'chan'), may hold values from -6 to 6
- offsets: int32 [8], P('dp'), may hold values from 0 to 127
- widths: int32 [8], P('dp'), may hold values from 32 to 64
- labels: int32 [8, 32, 128], P('dp'), may hold values from 0 to 19
- dw_kernel: bfloat16 [4, 9, 2048], P('section', None, 'chan'), may hold values from -2 to 2
- pw_weight: bfloat16 [4, 2048, 256], P('section', 'chan'), may hold values from -0.125 to 0.125
- pw_bias: float32 [4, 256], P('section', 'chan'), may hold values from -3 to 3
- proj: bfloat16 [4, 256, 256], P('section', 'chan'), may hold values from -0.1875 to 0.1875
- proj_bias: float32 [256], P('chan'), may hold values from -3 to 3
- upstream: bfloat16 [256, 8, 32, 128], P('chan', 'dp'), may hold values from -6 to 6
Outputs:
- aspp_out: bfloat16 [256, 8, 32, 128], P('chan', 'dp')
- input_grad: bfloat16 [8, 32, 128, 2048], P('dp', 'section', None, 'chan')
- grad_dw: float32 [4, 9, 2048], P('section', None, 'chan')
- grad_pw: float32 [4, 2048, 256], P('section', 'chan')
- grad_pw_bias: float32 [4, 256], P('section', 'chan')
- grad_proj: float32 [4, 256, 256], P('section', 'chan')
- grad_proj_bias: float32 [256], P('chan')
All inputs are finite; a program needn't handle non-finite values.
Results may differ from a plain program's by a relative error of at most 0.008.
Values may be sent and summed in bfloat16 or wider, within the bound.
No kernel may reach another device: no remote copies, remote signals or barrier semaphores. Data moves between devices by JAX's collectives and lax.ppermute only.
A program may use at most 128 MiB of HBM per device.

v0:
```python
import math
import jax
import jax.numpy as jnp
from jax import lax
from jax.sharding import PartitionSpec as P

RATE = 6
void_class = 19


def prefix(shard, axis, combine, identity):
    devices, place = (lax.axis_size(axis), lax.axis_index(axis))
    everything = lax.all_gather(shard, axis)
    start = jnp.broadcast_to(jnp.asarray(identity, shard.dtype), shard.shape)

    def step(k, before):
        reached = k < place
        new = combine(before, everything[k])
        return jnp.where(reached, new, before)

    return lax.fori_loop(0, devices, step, start)


def spread(value, axis, source):
    kept = jnp.where(lax.axis_index(axis) == source, value, 0).astype(value.dtype)
    return lax.psum(kept, axis)


def column_band(offsets, widths, col_count):
    columns = jnp.arange(col_count, dtype=jnp.int32)
    return jnp.mod(columns[None, :] - offsets[:, None], col_count) < widths[:, None]


def swish_slope(value):
    sig = jax.nn.sigmoid(value)
    return sig * (1.0 + value * (1.0 - sig))


def add_terms(earlier, latter):
    return earlier + latter


def local(feats, offsets, widths, labels, dw_kernel, pw_weight, pw_bias, proj, proj_bias, upstream):
    frame_count, row_count, col_count, chan_count = feats.shape
    segments = lax.axis_size("section")
    dilation = RATE * lax.axis_index("section")
    margin = RATE * (segments - 1)
    keep = column_band(offsets, widths, col_count)
    masked = feats * keep[:, None, :, None].astype(jnp.bfloat16)
    padded = jnp.pad(masked, ((0, 0), (margin, margin), (margin, margin), (0, 0)))
    kernel = dw_kernel[0].astype(jnp.float32)
    pixel_count = frame_count * row_count * col_count
    scaling = 1.0 / math.sqrt(pixel_count * lax.axis_size("dp"))

    def tap_slice(source, tap_index, direction):
        row_step = tap_index // 3 - 1
        col_step = tap_index % 3 - 1
        anchor = (
            0,
            margin + direction * dilation * row_step,
            margin + direction * dilation * col_step,
            0,
        )
        return lax.dynamic_slice(source, anchor, (frame_count, row_count, col_count, chan_count))

    accum = jnp.zeros((frame_count, row_count, col_count, chan_count), jnp.float32)
    for tap_index in range(9):
        accum = accum + tap_slice(padded, tap_index, 1).astype(jnp.float32) * kernel[tap_index]
    depth_out = accum.astype(jnp.bfloat16)
    depth_rows = depth_out.reshape(pixel_count, chan_count)
    weight = pw_weight[0]
    branch_share = pw_bias.shape[1]
    columns = weight
    preact = (
        lax.psum_scatter(
            lax.dot_general(
                columns, depth_rows, (((0,), (1,)), ((), ())), preferred_element_type=jnp.float32
            ),
            "chan",
            scatter_dimension=0,
            tiled=True,
        )
        + pw_bias[0][:, None]
    )
    branch_act = jax.nn.silu(preact).astype(jnp.bfloat16)
    proj_local = proj[0]
    columns = proj_local
    zpart = lax.psum_scatter(
        lax.dot_general(
            columns, branch_act, (((0,), (0,)), ((), ())), preferred_element_type=jnp.float32
        ),
        "chan",
        scatter_dimension=0,
        tiled=True,
    )
    up_rows = upstream.reshape(branch_share, pixel_count).astype(jnp.float32)
    labeled = (labels != void_class).reshape(pixel_count).astype(jnp.float32)
    before = prefix(zpart, "section", add_terms, jnp.zeros_like(zpart))
    zvalue = before + zpart + proj_bias[:, None]
    result = jax.nn.silu(zvalue).astype(jnp.bfloat16)
    gradient = (up_rows * swish_slope(zvalue) * labeled[None, :]).astype(jnp.bfloat16)
    result, out_grad = (result, gradient)
    result, out_grad = (
        spread(result, "section", segments - 1),
        spread(out_grad, "section", segments - 1),
    )
    proj_bias_grad = jnp.sum(out_grad.astype(jnp.float32), axis=1) * scaling
    shard_rows = lax.all_gather(out_grad, "chan", axis=0, tiled=True)
    act_grad = jnp.dot(proj_local, shard_rows, preferred_element_type=jnp.float32)
    piece_grad = lax.dot_general(
        branch_act, shard_rows, (((1,), (1,)), ((), ())), preferred_element_type=jnp.float32
    )
    proj_grad = piece_grad
    act_grad, proj_grad = (act_grad, proj_grad)
    pre_grad = (act_grad * swish_slope(preact)).astype(jnp.bfloat16)
    pw_bias_grad = jnp.sum(pre_grad.astype(jnp.float32), axis=1) * scaling
    shard_rows = lax.all_gather(pre_grad, "chan", axis=0, tiled=True)
    columns = weight
    depth_acc = lax.dot_general(
        shard_rows, columns, (((0,), (1,)), ((), ())), preferred_element_type=jnp.float32
    )
    piece_grad = lax.dot_general(
        depth_rows, shard_rows, (((0,), (1,)), ((), ())), preferred_element_type=jnp.float32
    )
    weight_grad = piece_grad
    depth_acc, weight_grad = (depth_acc, weight_grad)
    depth_grad = depth_acc.astype(jnp.bfloat16).reshape(
        frame_count, row_count, col_count, chan_count
    )
    padded_grad = jnp.pad(depth_grad, ((0, 0), (margin, margin), (margin, margin), (0, 0)))
    depth_f = depth_grad.astype(jnp.float32)
    input_term = jnp.zeros((frame_count, row_count, col_count, chan_count), jnp.float32)
    tap_grads = []
    for tap_index in range(9):
        source = tap_slice(padded, tap_index, 1).astype(jnp.float32)
        tap_grads.append(jnp.sum(source * depth_f, axis=(0, 1, 2)) * scaling)
        input_term = (
            input_term
            + tap_slice(padded_grad, tap_index, -1).astype(jnp.float32) * kernel[tap_index]
        )
    kernel_grad = jnp.stack(tap_grads)
    input_rows = lax.psum_scatter(input_term, "section", scatter_dimension=1, tiled=True)
    input_grad = (input_rows * keep[:, None, :, None].astype(jnp.float32)).astype(jnp.bfloat16)
    kernel_grad, weight_grad, pw_bias_grad, proj_grad, proj_bias_grad = lax.psum(
        (kernel_grad, weight_grad * scaling, pw_bias_grad, proj_grad * scaling, proj_bias_grad),
        "dp",
    )
    aspp_out = result.reshape(branch_share, frame_count, row_count, col_count)
    return (
        aspp_out,
        input_grad,
        kernel_grad[None],
        weight_grad[None],
        pw_bias_grad[None],
        proj_grad[None],
        proj_bias_grad,
    )


def solution(mesh):
    in_specs = (
        P("dp", None, None, "chan"),
        P("dp"),
        P("dp"),
        P("dp", None, None),
        P("section", None, "chan"),
        P("section", "chan", None),
        P("section", "chan"),
        P("section", "chan", None),
        P("chan"),
        P("chan", "dp", None, None),
    )
    out_specs = (
        P("chan", "dp", None, None),
        P("dp", "section", None, "chan"),
        P("section", None, "chan"),
        P("section", "chan", None),
        P("section", "chan"),
        P("section", "chan", None),
        P("chan"),
    )
    return jax.shard_map(local, mesh=mesh, in_specs=in_specs, out_specs=out_specs, check_vma=False)
```

profile of v0, /device:TPU:2, one launch (start us, length us, event | category | flops | bytes accessed | tf_op | source)
XLA Modules:
  0.0 520.5 jit_solution(6234613447369685872)
XLA Ops:
  8.7 1.8 broadcast_multiply_fusion
  10.5 1.3 copy-done.1
  11.8 16.0 %fusion.10 = bf16[2,32,128,128]{3,2,1,0:T(8,128)(2,1)S(1)} fusion(bf16[2,32,128,128]{3,2,1,0:T(8,128)(2,1)S(1)} %broadcast_multiply_fusion, f32[128]{0:T(128)S(1)} %get-tuple-element.153, f32[128]{0:T(128)S(1)} %get-tuple-element.154, f32[128]{0:T(128)S(1)} %get-tuple-element.155, f32[128]{0:T(128)S(1)} %get-tuple-element.156, ...), kind=kLoop, calls=%fused_computation.50 | loop fusion | flops 28311552 | bytes 4198928 | tf_op jit(solution)/shard_map/convert_element_type | solution.py:69
  27.8 4.5 convolution_bitcast_fusion.1
  32.3 8.9 %copy.33 = f32[256,8192]{1,0:T(8,128)} copy(f32[256,8192]{0,1:T(8,128)} %convolution_bitcast_fusion.1) | data formatting | bytes 16777216
  41.5 73.4 %reduce-scatter.11.cloned.1.call-done = f32[16,8192]{1,0:T(8,128)} async-done(((f32[256,8192]{1,0:T(8,128)}), f32[16,8192]{1,0:T(8,128)}) %reduce-scatter.11.cloned.1.call-update) | async-done | bytes 524304 | tf_op jit(solution)/shard_map/reduce_scatter | solution.py:75
  114.9 5.6 %convolution_bitcast_fusion = f32[256,8192]{0,1:T(8,128)} fusion(bf16[1,16,256]{2,1,0:T(8,128)(2,1)S(1)} %copy-done.7, f32[16,8192]{1,0:T(8,128)} %reduce-scatter.11.cloned.1.call-done, f32[16]{0:T(128)S(1)} %bitcast.133), kind=kOutput, calls=%fused_computation.27 | convolution fusion | flops 67895296 | bytes 8921152 | tf_op jit(solution)/shard_map/dot_general | solution.py:89
  120.6 8.9 %copy.35 = f32[256,8192]{1,0:T(8,128)} copy(f32[256,8192]{0,1:T(8,128)} %convolution_bitcast_fusion) | data formatting | bytes 16777216
  129.6 69.4 %reduce-scatter.13.cloned.1.call-done = f32[16,8192]{1,0:T(8,128)} async-done(((f32[256,8192]{1,0:T(8,128)}), f32[16,8192]{1,0:T(8,128)}) %reduce-scatter.13.cloned.1.call-update) | async-done | bytes 524304 | tf_op jit(solution)/shard_map/reduce_scatter | solution.py:88
  199.0 0.8 convert.2
  199.9 32.1 %all-gather.9.cloned.1.call-done = f32[64,8192]{1,0:T(8,128)} async-done(((f32[16,8192]{1,0:T(8,128)}), f32[64,8192]{1,0:T(8,128)}) %all-gather.9.cloned.1.call-update) | async-done | bytes 2097168 | tf_op jit(solution)/shard_map/all_gather | solution.py:13
  232.0 4.9 while.14
  232.0 1.3 add_select_fusion.2
  233.3 1.2 add_select_fusion.2
  234.5 1.2 add_select_fusion.2
  235.7 1.2 add_select_fusion.2
  236.9 2.4 broadcast_select_fusion
  240.2 48.3 %all-reduce.9.cloned.1.call-done = (bf16[16,2,32,128]{3,2,1,0:T(8,128)(2,1)}, bf16[16,8192]{1,0:T(8,128)(2,1)}) async-done(((bf16[16,2,32,128]{3,2,1,0:T(8,128)(2,1)}, bf16[16,8192]{1,0:T(8,128)(2,1)}), (bf16[16,2,32,128]{3,2,1,0:T(8,128)(2,1)}, bf16[16,8192]{1,0:T(8,128)(2,1)})) %all-reduce.9.cloned.1.call-update) | async-done | bytes 524304 | tf_op jit(solution)/shard_map/psum | solution.py:26
  288.5 45.4 %all-gather.5.cloned.1.call-done = bf16[256,8192]{1,0:T(8,128)(2,1)} async-done(((bf16[16,8192]{1,0:T(8,128)(2,1)}), bf16[256,8192]{1,0:T(8,128)(2,1)}) %all-gather.5.cloned.1.call-update) | async-done | bytes 4194320 | tf_op jit(solution)/shard_map/all_gather | solution.py:108
  333.9 3.7 convert_reduce_fusion.1
  337.6 40.8 %all-gather.7.cloned.1.call-done = bf16[256,8192]{1,0:T(8,128)(2,1)} async-done(((bf16[16,8192]{1,0:T(8,128)(2,1)}), bf16[256,8192]{1,0:T(8,128)(2,1)}) %all-gather.7.cloned.1.call-update) | async-done | bytes 4194320 | tf_op jit(solution)/shard_map/all_gather | solution.py:117
  378.4 16.1 %fusion.24 = (f32[128]{0:T(128)S(1)}, f32[128]{0:T(128)S(1)}, f32[128]{0:T(128)S(1)}, f32[128]{0:T(128)S(1)}, f32[128]{0:T(128)S(1)}, /*index=5*/f32[128]{0:T(12...) fusion(s32[]{:T(128)S(6)} %select_n.96, s32[]{:T(128)S(6)} %select_n.95, ...), kind=kOutput, calls=%fused_computation.64 | convolution fusion | flops 567278464 | bytes 8458768 | tf_op jit(solution)/shard_map/dot_general | solution.py:119
  394.5 16.2 %fusion.15 = f32[2,32,128,128]{3,2,1,0:T(8,128)S(1)} fusion(bf16[2,32,128,128]{3,2,1,0:T(8,128)(2,1)S(1)} %bitcast.127, s32[]{:T(128)S(6)} %select_n.96, s32[]{:T(128)S(6)} %select_n.95, s32[]{:T(128)S(6)} %select_n.94, s32[]{:T(128)S(6)} %select_n.93, f32[128]{0:T(128)S(1)} %get-tuple-element.153, f32[128]{0:T(128)S(1)} %get-tuple-element.154, ...), kind=kLoop, calls=%fused_computation.55 | loop fusion | flops 27262976 | bytes 6296080 | tf_op jit(solution)/shard_map/add | solution.py:138
  411.0 4.4 copy.50
  416.5 3.4 fusion.26
  420.0 17.6 %all-reduce.2 = (f32[1,9,128]{2,1,0:T(8,128)S(1)}, f32[1,16]{1,0:T(1,128)}, f32[1,16,256]{2,1,0:T(8,128)}, f32[16]{0:T(128)}) all-reduce(f32[1,9,128]{2,1,0:T(8,128)S(1)} %bitcast.132, f32[1,16]{1,0:T(1,128)S(1)} %multiply_bitcast_fusion, f32[1,16,256]{2,1,0:T(8,128)S(1)} %fusion.26, ...), channel_id=1, replica_groups=mesh['section'=4,'dp'=4,'chan'=16] {'dp'}, use_global_device_ids=true, to_apply=%region_16.17 | all-reduce | flops 5280 | bytes 42240 | tf_op jit(solution)/shard_map/psum | solution.py:144
  438.3 4.5 fusion.25
  442.8 18.3 %reduce-scatter.15.cloned.1.call-done = f32[8,32768]{1,0:T(8,128)} async-done(((f32[32,32768]{1,0:T(8,128)}), f32[8,32768]{1,0:T(8,128)}) %reduce-scatter.15.cloned.1.call-update) | async-done | bytes 1048592
  461.1 1.4 copy.42
  462.5 1.0 fusion.27
  463.5 47.9 %all-reduce.7.cloned.1.call-done = f32[1,128,256]{2,1,0:T(8,128)} async-done(((f32[1,128,256]{2,1,0:T(8,128)}), f32[1,128,256]{2,1,0:T(8,128)}) %all-reduce.7.cloned.1.call-update) | async-done | bytes 131088 | tf_op jit(solution)/shard_map/psum | solution.py:144
  512.1 1.6 copy.61
  (53 shorter events, 5.6 us)
Async XLA Ops:
  7.2 20.7 %copy-start = (bf16[1,128,256]{2,1,0:T(8,128)(2,1)S(1)}, bf16[1,128,256]{2,1,0:T(8,128)(2,1)}, u32[]{:S(2)}) copy-start(bf16[1,128,256]{2,1,0:T(8,128)(2,1)} %param.17) | copy-start | bytes 196612
  7.2 107.7 %reduce-scatter.11.cloned.1.call-start = ((), (), s32[]{:S(2)}) async-start(), calls=%async_computation.7 | async-start | bytes 8912896 | tf_op jit(solution)/shard_map/reduce_scatter | solution.py:75
  10.5 1.4 copy-start.1
  41.2 73.7 %copy-start.7 = (bf16[1,16,256]{2,1,0:T(8,128)(2,1)S(1)}, bf16[1,16,256]{2,1,0:T(8,128)(2,1)}, u32[]{:S(2)}) copy-start(bf16[1,16,256]{2,1,0:T(8,128)(2,1)} %param.19) | copy-start | bytes 24580
  41.2 73.7 %copy-start.8 = (f32[1,16]{1,0:T(1,128)S(1)}, f32[1,16]{1,0:T(1,128)}, u32[]{:S(2)}) copy-start(f32[1,16]{1,0:T(1,128)} %param.18) | copy-start | bytes 196
  41.2 157.7 %reduce-scatter.13.cloned.1.call-start = ((), (), s32[]{:S(2)}) async-start(), calls=%async_computation.8 | async-start | bytes 8912896 | tf_op jit(solution)/shard_map/reduce_scatter | solution.py:88
  129.5 69.5 %copy-start.4 = (bf16[16,2,32,128]{3,2,1,0:T(8,128)(2,1)S(1)}, bf16[16,2,32,128]{3,2,1,0:T(8,128)(2,1)}, u32[]{:S(2)}) copy-start(bf16[16,2,32,128]{3,2,1,0:T(8,128)(2,1)} %param.21) | copy-start | bytes 786436
  129.5 70.4 %copy-start.6 = (s32[2,32,128]{2,1,0:T(8,128)S(1)}, s32[2,32,128]{2,1,0:T(8,128)}, u32[]{:S(2)}) copy-start(s32[2,32,128]{2,1,0:T(8,128)} %param.15) | copy-start | bytes 98308
  129.5 102.5 %all-gather.9.cloned.1.call-start = ((), (), s32[]{:S(2)}) async-start(), calls=%async_computation.6 | async-start | bytes 2621440 | tf_op jit(solution)/shard_map/all_gather | solution.py:13
  199.0 89.5 %all-reduce.9.cloned.1.call-start = ((), (), s32[]{:S(2)}) async-start(), calls=%async_computation.10 | async-start | bytes 1048576 | tf_op jit(solution)/shard_map/psum | solution.py:26
  199.9 37.0 %copy-start.9 = (f32[16]{0:T(128)S(1)}, f32[16]{0:T(128)}, u32[]{:S(2)}) copy-start(f32[16]{0:T(128)} %param.20) | copy-start | bytes 196
  232.0 101.9 %copy-start.2 = (f32[16,8192]{1,0:T(8,128)S(1)}, f32[16,8192]{1,0:T(8,128)}, u32[]{:S(2)}) copy-start(f32[16,8192]{1,0:T(8,128)} %reduce-scatter.11.cloned.1.call-done) | copy-start | bytes 1572868
  240.1 93.8 %all-gather.5.cloned.1.call-start = ((), (), s32[]{:S(2)}) async-start(), calls=%async_computation.3 | async-start | bytes 4456448 | tf_op jit(solution)/shard_map/all_gather | solution.py:108
  288.5 90.0 %all-gather.7.cloned.1.call-start = ((), (), s32[]{:S(2)}) async-start(), calls=%async_computation.4 | async-start | bytes 4456448 | tf_op jit(solution)/shard_map/all_gather | solution.py:117
  337.6 123.5 %reduce-scatter.15.cloned.1.call-start = ((), (), s32[]{:S(2)}) async-start(), calls=%async_computation.9 | async-start | bytes 5242880
  415.4 0.9 copy-start.3
  415.4 95.9 %all-reduce.7.cloned.1.call-start = ((), (), s32[]{:S(2)}) async-start(), calls=%async_computation.5 | async-start | bytes 262144 | tf_op jit(solution)/shard_map/psum | solution.py:144
  438.3 73.1 %copy-start.5 = (bf16[16,2,32,128]{3,2,1,0:T(8,128)(2,1)S(1)}, bf16[16,2,32,128]{3,2,1,0:T(8,128)(2,1)}, u32[]{:S(2)}) copy-start(bf16[16,2,32,128]{3,2,1,0:T(8,128)(2,1)} %get-tuple-element.217) | copy-start | bytes 786436
Sparse Core Ops, SparseCore 0:
  41.4 73.4 reduce-scatter.10
  129.6 69.2 reduce-scatter.12
  200.8 31.1 all-gather.8
  240.2 48.1 all-reduce.8
  290.1 43.7 all-gather.4
  337.7 40.6 all-gather.6
  415.5 45.4 reduce-scatter.14
  464.0 47.2 all-reduce.6
where the time goes:
time: 521 us; the launch traced here: 520 us
  waiting for transfers between devices  376 us (72%)
  other arithmetic  44.7 us (9%)
  matrix products  37.7 us (7%)
  local copies, waits for them, and re-layouts  29.6 us (6%)
  blocking collectives  17.6 us (3%)
  between operations  14.3 us (3%)
    reduce_scatter x1, waiting for transfers between devices, local(): lax.psum_scatter(lax.dot_general(columns, depth_rows, (((0,), (1,)), ((),...  73.4 us
    reduce_scatter x1, waiting for transfers between devices, local(): lax.psum_scatter(lax.dot_general(columns, branch_act, (((0,), (0,)), ((),...  69.4 us
    psum x1, waiting for transfers between devices, spread(): return lax.psum(kept, axis)  48.3 us
    psum x1, waiting for transfers between devices, local(): lax.psum((kernel_grad, weight_grad * scaling, pw_bias_grad, proj_grad * s...  47.9 us
    all_gather x1, waiting for transfers between devices, local(): shard_rows = lax.all_gather(out_grad, 'chan', axis=0, tiled=True)  45.4 us
    all_gather x1, waiting for transfers between devices, local(): shard_rows = lax.all_gather(pre_grad, 'chan', axis=0, tiled=True)  40.8 us
    all_gather x1, waiting for transfers between devices, prefix(): everything = lax.all_gather(shard, axis)  32.1 us
    unnamed x29, local copies, waits for them, and re-layouts  29.6 us
  transfers between devices with their start and end apart: 8, of which 8 were waited for; matrix products, arithmetic and copies ran while one was open for 2% of the time, Pallas kernels for 0%

commit v1 on v0

--- a/solution.py
+++ b/solution.py
@@ -23,7 +23,7 @@
 
 def spread(value, axis, source):
     kept = jnp.where(lax.axis_index(axis) == source, value, 0).astype(value.dtype)
-    return lax.psum(kept, axis)
+    return lax.all_gather(kept, axis).sum(axis=0)
 
 
 def column_band(offsets, widths, col_count):

time: 521 us -> 498 us (0.956)
  waiting for transfers between devices: 376 us -> 351 us
    psum x1 -> x0, waiting for transfers between devices: 48.3 us -> none  [spread(): return lax.psum(kept, axis)]
    all_gather x0 -> x2, waiting for transfers between devices: none -> 26.7 us  [spread(): return lax.all_gather(kept, axis).sum(axis=0)]
    unnamed x29 -> x26, local copies, waits for them, and re-layouts: 29.6 us -> 28.3 us
    unnamed x9 -> x10, waiting for transfers between devices: 18.4 us -> 17.6 us
  transfers between devices with their start and end apart: 8 -> 9, of which waited for: 8 -> 8; matrix products, arithmetic and copies ran while one was open for 2% -> 10% of each run, Pallas kernels for 0% -> 0%
where the time goes in v1:
time: 498 us; the launch traced here: 497 us
  waiting for transfers between devices  351 us (70%)
  other arithmetic  48.4 us (10%)
  matrix products  37.6 us (8%)
  local copies, waits for them, and re-layouts  28.3 us (6%)
  blocking collectives  17.6 us (4%)
  between operations  14 us (3%)
    reduce_scatter x1, waiting for transfers between devices, local(): lax.psum_scatter(lax.dot_general(columns, depth_rows, (((0,), (1,)), ((),...  73.3 us
    reduce_scatter x1, waiting for transfers between devices, local(): lax.psum_scatter(lax.dot_general(columns, branch_act, (((0,), (0,)), ((),...  69.5 us
    psum x1, waiting for transfers between devices, local(): lax.psum((kernel_grad, weight_grad * scaling, pw_bias_grad, proj_grad * s...  47.9 us
    all_gather x1, waiting for transfers between devices, local(): shard_rows = lax.all_gather(out_grad, 'chan', axis=0, tiled=True)  43.5 us
    all_gather x1, waiting for transfers between devices, local(): shard_rows = lax.all_gather(pre_grad, 'chan', axis=0, tiled=True)  40 us
    all_gather x1, waiting for transfers between devices, prefix(): everything = lax.all_gather(shard, axis)  32.1 us
    unnamed x26, local copies, waits for them, and re-layouts  28.3 us
    all_gather x2, waiting for transfers between devices, spread(): return lax.all_gather(kept, axis).sum(axis=0)  26.7 us
  transfers between devices with their start and end apart: 9, of which 8 were waited for; matrix products, arithmetic and copies ran while one was open for 10% of the time, Pallas kernels for 0%

profile of v1, /device:TPU:2, one launch (start us, length us, event | category | flops | bytes accessed | tf_op | source)
XLA Modules:
  0.0 497.5 jit_solution(11057854716876976411)
XLA Ops:
  8.7 1.8 broadcast_multiply_fusion
  10.5 1.3 copy-done.1
  11.8 16.0 %fusion.10 = bf16[2,32,128,128]{3,2,1,0:T(8,128)(2,1)S(1)} fusion(bf16[2,32,128,128]{3,2,1,0:T(8,128)(2,1)S(1)} %broadcast_multiply_fusion, f32[128]{0:T(128)S(1)} %get-tuple-element.158, f32[128]{0:T(128)S(1)} %get-tuple-element.159, f32[128]{0:T(128)S(1)} %get-tuple-element.160, f32[128]{0:T(128)S(1)} %get-tuple-element.161, ...), kind=kLoop, calls=%fused_computation.50 | loop fusion | flops 28311552 | bytes 4198928 | tf_op jit(solution)/shard_map/convert_element_type | solution.py:69
  27.8 4.5 convolution_bitcast_fusion.1
  32.3 8.9 %copy.37 = f32[256,8192]{1,0:T(8,128)} copy(f32[256,8192]{0,1:T(8,128)} %convolution_bitcast_fusion.1) | data formatting | bytes 16777216
  41.5 73.3 %reduce-scatter.11.cloned.1.call-done = f32[16,8192]{1,0:T(8,128)} async-done(((f32[256,8192]{1,0:T(8,128)}), f32[16,8192]{1,0:T(8,128)}) %reduce-scatter.11.cloned.1.call-update) | async-done | bytes 524304 | tf_op jit(solution)/shard_map/reduce_scatter | solution.py:75
  114.8 5.6 %convolution_bitcast_fusion = f32[256,8192]{0,1:T(8,128)} fusion(bf16[1,16,256]{2,1,0:T(8,128)(2,1)S(1)} %copy-done.6, f32[16,8192]{1,0:T(8,128)} %reduce-scatter.11.cloned.1.call-done, f32[16]{0:T(128)S(1)} %bitcast.137), kind=kOutput, calls=%fused_computation.27 | convolution fusion | flops 67895296 | bytes 8921152 | tf_op jit(solution)/shard_map/dot_general | solution.py:89
  120.5 8.9 %copy.39 = f32[256,8192]{1,0:T(8,128)} copy(f32[256,8192]{0,1:T(8,128)} %convolution_bitcast_fusion) | data formatting | bytes 16777216
  129.5 69.5 %reduce-scatter.13.cloned.1.call-done = f32[16,8192]{1,0:T(8,128)} async-done(((f32[256,8192]{1,0:T(8,128)}), f32[16,8192]{1,0:T(8,128)}) %reduce-scatter.13.cloned.1.call-update) | async-done | bytes 524304 | tf_op jit(solution)/shard_map/reduce_scatter | solution.py:88
  199.9 32.1 %all-gather.13.cloned.1.call-done = f32[64,8192]{1,0:T(8,128)} async-done(((f32[16,8192]{1,0:T(8,128)}), f32[64,8192]{1,0:T(8,128)}) %all-gather.13.cloned.1.call-update) | async-done | bytes 2097168 | tf_op jit(solution)/shard_map/all_gather | solution.py:13
  232.0 4.9 while.14
  232.0 1.3 add_select_fusion.2
  233.3 1.2 add_select_fusion.2
  234.5 1.2 add_select_fusion.2
  235.7 1.2 add_select_fusion.2
  237.0 2.5 broadcast_select_fusion
  239.5 26.7 %all-gather.17.cloned.1.call-done = bf16[64,8192]{1,0:T(8,128)(2,1)} async-done(((bf16[16,8192]{1,0:T(8,128)(2,1)}), bf16[64,8192]{1,0:T(8,128)(2,1)}) %all-gather.17.cloned.1.call-update) | async-done | bytes 1048592 | tf_op jit(solution)/shard_map/all_gather | solution.py:26
  266.2 2.1 reduce_sum.124
  268.4 43.5 %all-gather.9.cloned.1.call-done = bf16[256,8192]{1,0:T(8,128)(2,1)} async-done(((bf16[16,8192]{1,0:T(8,128)(2,1)}), bf16[256,8192]{1,0:T(8,128)(2,1)}) %all-gather.9.cloned.1.call-update) | async-done | bytes 4194320 | tf_op jit(solution)/shard_map/all_gather | solution.py:108
  311.9 3.7 convert_reduce_fusion.1
  316.4 40.0 %all-gather.11.cloned.1.call-done = bf16[256,8192]{1,0:T(8,128)(2,1)} async-done(((bf16[16,8192]{1,0:T(8,128)(2,1)}), bf16[256,8192]{1,0:T(8,128)(2,1)}) %all-gather.11.cloned.1.call-update) | async-done | bytes 4194320 | tf_op jit(solution)/shard_map/all_gather | solution.py:117
  356.4 16.1 %fusion.24 = (f32[128]{0:T(128)S(1)}, f32[128]{0:T(128)S(1)}, f32[128]{0:T(128)S(1)}, f32[128]{0:T(128)S(1)}, f32[128]{0:T(128)S(1)}, /*index=5*/f32[128]{0:T(12...) fusion(s32[]{:T(128)S(6)} %select_n.96, s32[]{:T(128)S(6)} %select_n.95, ...), kind=kOutput, calls=%fused_computation.64 | convolution fusion | flops 567278464 | bytes 8458768 | tf_op jit(solution)/shard_map/dot_general | solution.py:119
  372.5 16.2 %fusion.15 = f32[2,32,128,128]{3,2,1,0:T(8,128)S(1)} fusion(bf16[2,32,128,128]{3,2,1,0:T(8,128)(2,1)S(1)} %bitcast.128, s32[]{:T(128)S(6)} %select_n.96, s32[]{:T(128)S(6)} %select_n.95, s32[]{:T(128)S(6)} %select_n.94, s32[]{:T(128)S(6)} %select_n.93, f32[128]{0:T(128)S(1)} %get-tuple-element.158, f32[128]{0:T(128)S(1)} %get-tuple-element.159, ...), kind=kLoop, calls=%fused_computation.55 | loop fusion | flops 27262976 | bytes 6296080 | tf_op jit(solution)/shard_map/add | solution.py:138
  389.0 4.4 copy.54
  393.7 1.5 reduce_sum.123
  396.2 3.4 fusion.26
  399.7 17.6 %all-reduce.2 = (f32[1,9,128]{2,1,0:T(8,128)S(1)}, f32[1,16]{1,0:T(1,128)}, f32[1,16,256]{2,1,0:T(8,128)}, f32[16]{0:T(128)}) all-reduce(f32[1,9,128]{2,1,0:T(8,128)S(1)} %bitcast.136, f32[1,16]{1,0:T(1,128)S(1)} %multiply_bitcast_fusion, f32[1,16,256]{2,1,0:T(8,128)S(1)} %fusion.26, ...), channel_id=1, replica_groups=mesh['section'=4,'dp'=4,'chan'=16] {'dp'}, use_global_device_ids=true, to_apply=%region_16.17 | all-reduce | flops 5280 | bytes 42240 | tf_op jit(solution)/shard_map/psum | solution.py:144
  417.9 4.4 fusion.25
  422.3 16.8 %reduce-scatter.15.cloned.1.call-done = f32[8,32768]{1,0:T(8,128)} async-done(((f32[32,32768]{1,0:T(8,128)}), f32[8,32768]{1,0:T(8,128)}) %reduce-scatter.15.cloned.1.call-update) | async-done | bytes 1048592
  439.1 1.4 copy.46
  441.5 47.9 %all-reduce.5.cloned.1.call-done = f32[1,128,256]{2,1,0:T(8,128)} async-done(((f32[1,128,256]{2,1,0:T(8,128)}), f32[1,128,256]{2,1,0:T(8,128)}) %all-reduce.5.cloned.1.call-update) | async-done | bytes 131088 | tf_op jit(solution)/shard_map/psum | solution.py:144
  489.4 1.6 copy.62
  (55 shorter events, 6.9 us)
Async XLA Ops:
  7.2 20.7 %copy-start = (bf16[1,128,256]{2,1,0:T(8,128)(2,1)S(1)}, bf16[1,128,256]{2,1,0:T(8,128)(2,1)}, u32[]{:S(2)}) copy-start(bf16[1,128,256]{2,1,0:T(8,128)(2,1)} %param.17) | copy-start | bytes 196612
  7.2 107.6 %reduce-scatter.11.cloned.1.call-start = ((), (), s32[]{:S(2)}) async-start(), calls=%async_computation.9 | async-start | bytes 8912896 | tf_op jit(solution)/shard_map/reduce_scatter | solution.py:75
  10.5 1.4 copy-start.1
  41.2 73.6 %copy-start.6 = (bf16[1,16,256]{2,1,0:T(8,128)(2,1)S(1)}, bf16[1,16,256]{2,1,0:T(8,128)(2,1)}, u32[]{:S(2)}) copy-start(bf16[1,16,256]{2,1,0:T(8,128)(2,1)} %param.19) | copy-start | bytes 24580
  41.2 73.6 %copy-start.7 = (f32[1,16]{1,0:T(1,128)S(1)}, f32[1,16]{1,0:T(1,128)}, u32[]{:S(2)}) copy-start(f32[1,16]{1,0:T(1,128)} %param.18) | copy-start | bytes 196
  41.2 157.7 %reduce-scatter.13.cloned.1.call-start = ((), (), s32[]{:S(2)}) async-start(), calls=%async_computation.10 | async-start | bytes 8912896 | tf_op jit(solution)/shard_map/reduce_scatter | solution.py:88
  129.4 69.6 %copy-start.4 = (bf16[16,2,32,128]{3,2,1,0:T(8,128)(2,1)S(1)}, bf16[16,2,32,128]{3,2,1,0:T(8,128)(2,1)}, u32[]{:S(2)}) copy-start(bf16[16,2,32,128]{3,2,1,0:T(8,128)(2,1)} %param.21) | copy-start | bytes 786436
  129.4 70.5 %copy-start.5 = (s32[2,32,128]{2,1,0:T(8,128)S(1)}, s32[2,32,128]{2,1,0:T(8,128)}, u32[]{:S(2)}) copy-start(s32[2,32,128]{2,1,0:T(8,128)} %param.15) | copy-start | bytes 98308
  129.4 102.6 %all-gather.13.cloned.1.call-start = ((), (), s32[]{:S(2)}) async-start(), calls=%async_computation.6 | async-start | bytes 2621440 | tf_op jit(solution)/shard_map/all_gather | solution.py:13
  199.0 67.2 %all-gather.17.cloned.1.call-start = ((), (), s32[]{:S(2)}) async-start(), calls=%async_computation.8 | async-start | bytes 1310720 | tf_op jit(solution)/shard_map/all_gather | solution.py:26
  199.9 37.1 %copy-start.8 = (f32[16]{0:T(128)S(1)}, f32[16]{0:T(128)}, u32[]{:S(2)}) copy-start(f32[16]{0:T(128)} %param.20) | copy-start | bytes 196
  232.0 79.9 %copy-start.2 = (f32[16,8192]{1,0:T(8,128)S(1)}, f32[16,8192]{1,0:T(8,128)}, u32[]{:S(2)}) copy-start(f32[16,8192]{1,0:T(8,128)} %reduce-scatter.11.cloned.1.call-done) | copy-start | bytes 1572868
  239.4 72.4 %all-gather.9.cloned.1.call-start = ((), (), s32[]{:S(2)}) async-start(), calls=%async_computation.3 | async-start | bytes 4456448 | tf_op jit(solution)/shard_map/all_gather | solution.py:108
  268.4 88.0 %all-gather.11.cloned.1.call-start = ((), (), s32[]{:S(2)}) async-start(), calls=%async_computation.4 | async-start | bytes 4456448 | tf_op jit(solution)/shard_map/all_gather | solution.py:117
  315.6 78.2 %all-gather.15.cloned.1.call-start = ((), (), s32[]{:S(2)}) async-start(), calls=%async_computation.7 | async-start | bytes 1310720 | tf_op jit(solution)/shard_map/all_gather | solution.py:26
  316.3 122.7 %reduce-scatter.15.cloned.1.call-start = ((), (), s32[]{:S(2)}) async-start(), calls=%async_computation.11 | async-start | bytes 5242880
  393.4 2.6 copy-start.3
  393.4 95.9 %all-reduce.5.cloned.1.call-start = ((), (), s32[]{:S(2)}) async-start(), calls=%async_computation.5 | async-start | bytes 262144 | tf_op jit(solution)/shard_map/psum | solution.py:144
Sparse Core Ops, SparseCore 0:
  41.4 73.4 reduce-scatter.10
  129.6 69.3 reduce-scatter.12
  200.8 31.2 all-gather.12
  239.6 26.5 all-gather.16
  268.5 43.3 all-gather.8
  315.7 40.6 all-gather.10
  358.2 24.1 all-gather.14
  393.5 45.4 reduce-scatter.14
  442.1 47.2 all-reduce.4
